TPU v7x, 512 devices: a whole 4x4x16 slice. The times are simulated.
512 devices in a mesh: dp: 64 (over y_lo, z, core), blk: 8 (over y_hi, x).
Axes of the slice: x: 4, y: 4 (y_hi: 2, y_lo: 2; y = y_hi * 2 + y_lo), z: 16, core: 2. Of those that a mesh axis runs over, the one named last changes fastest.
Arguments:
- resid: bfloat16 [2048, 2048], P('dp'), may hold values from -40 to 40
- queries: bfloat16 [2048, 16, 128], P('dp', 'blk'), may hold values from -60 to 60
- new_kv: bfloat16 [2048, 2, 8, 128], P('dp', None, 'blk'), may hold values from -6 to 6
- prefix_pool: bfloat16 [2048, 128, 2, 8, 128], P('dp', None, None, 'blk'), may hold values from -6 to 6
- page_table: int32 [64, 32], P('dp'), may hold values from 0 to 31, each once within a row
- prompt_len: int32 [64], P('dp'), may hold values from 1 to 4096, 131072 in all
- tail_pool: bfloat16 [1024, 128, 2, 8, 128], P('dp', None, None, 'blk'), may hold values from -6 to 6
- tail_len: int32 [64, 16], P('dp'), may hold values from 1 to 128, 1024 in all within a row
- migration: int32 [1024], replicated, may hold values from 0 to 1023, each once
- out_w: bfloat16 [2048, 2048], P('blk'), may hold values from -0.125 to 0.125
- mlp_gain: bfloat16 [2048], replicated, may hold values from 0.099609375 to 1.8984375
- gate_w: bfloat16 [2048, 6144], P('blk', 'dp'), may hold values from -0.125 to 0.125
- up_w: bfloat16 [2048, 6144], P('blk', 'dp'), may hold values from -0.125 to 0.125
- down_w: bfloat16 [6144, 2048], P('dp', 'blk'), may hold values from -0.078125 to 0.078125
- final_gain: bfloat16 [2048], P('blk'), may hold values from 0.099609375 to 1.8984375
- score_w: bfloat16 [2048], P('blk'), may hold values from -0.125 to 0.125
Outputs:
- hidden_out: bfloat16 [2048, 2048], P('dp', 'blk')
- score: float32 [2048], P('dp')
Inputs may be any that keep to these rules, and one draw needn't show every extreme that they name: `page_table`: each row lists every page of the device's pool once. `migration`: names every continuation once.
All inputs are finite; a program needn't handle non-finite values. No bound on the sum of `prompt_len` on one device may be relied on, other than what follows from the above.
Results may differ from a plain program's by a relative error of at most 0.012.
Values may be sent and summed in bfloat16 or wider, within the bound.
A program may use at most 64 MiB of HBM per device.

v0:
```python
import math
import jax
import jax.numpy as jnp
from jax import lax
from jax.sharding import PartitionSpec as P

D = 2048
NEW = 2
NEG = -1e30
EPS = 1e-06


def attend_prompt(queries, pool, table, prompt_len, tails, tail_len, pairs):
    token_rows, heads, width = queries.shape
    groups = pairs.shape[2]
    repeat = heads // groups
    conts = tails.shape[0]
    fresh = token_rows // conts
    prefix = jnp.take(pool, table, axis=0).reshape(-1, 2, groups, width)
    span = prefix.shape[0]
    grouped = queries.reshape(conts, fresh, groups, repeat, width)
    recent = pairs.reshape(conts, fresh, 2, groups, width)
    factor = 1.0 / math.sqrt(width)
    pre_scores = (
        jnp.einsum("cngrd,pgd->gcnrp", grouped, prefix[:, 0], preferred_element_type=jnp.float32)
        * factor
    )
    tail_scores = (
        jnp.einsum("cngrd,ctgd->gcnrt", grouped, tails[:, :, 0], preferred_element_type=jnp.float32)
        * factor
    )
    new_scores = (
        jnp.einsum(
            "cngrd,cmgd->gcnrm", grouped, recent[:, :, 0], preferred_element_type=jnp.float32
        )
        * factor
    )
    pre_mask = (jnp.arange(span) < prompt_len)[None, None, None, None, :]
    tail_mask = (jnp.arange(tails.shape[1])[None, :] < tail_len[:, None])[None, :, None, None, :]
    new_mask = (jnp.arange(fresh)[None, :] <= jnp.arange(fresh)[:, None])[None, None, :, None, :]
    pre_scores = jnp.where(pre_mask, pre_scores, NEG)
    tail_scores = jnp.where(tail_mask, tail_scores, NEG)
    new_scores = jnp.where(new_mask, new_scores, NEG)
    highest = jnp.maximum(
        jnp.maximum(jnp.max(pre_scores, -1), jnp.max(tail_scores, -1)), jnp.max(new_scores, -1)
    )[..., None]
    pre_weights = jnp.where(pre_mask, jnp.exp(pre_scores - highest), 0.0)
    tail_weights = jnp.where(tail_mask, jnp.exp(tail_scores - highest), 0.0)
    new_weights = jnp.where(new_mask, jnp.exp(new_scores - highest), 0.0)
    total = jnp.sum(pre_weights, -1) + jnp.sum(tail_weights, -1) + jnp.sum(new_weights, -1)
    mixed = jnp.einsum(
        "gcnrp,pgd->cngrd",
        pre_weights.astype(jnp.bfloat16),
        prefix[:, 1],
        preferred_element_type=jnp.float32,
    )
    mixed = mixed + jnp.einsum(
        "gcnrt,ctgd->cngrd",
        tail_weights.astype(jnp.bfloat16),
        tails[:, :, 1],
        preferred_element_type=jnp.float32,
    )
    mixed = mixed + jnp.einsum(
        "gcnrm,cmgd->cngrd",
        new_weights.astype(jnp.bfloat16),
        recent[:, :, 1],
        preferred_element_type=jnp.float32,
    )
    mixed = mixed / jnp.transpose(total, (1, 2, 0, 3))[..., None]
    return mixed.reshape(token_rows, heads * width).astype(jnp.bfloat16)


def shards(
    resid,
    queries,
    new_kv,
    prefix_pool,
    page_table,
    prompt_len,
    tail_pool,
    tail_len,
    migration,
    out_w,
    mlp_gain,
    gate_w,
    up_w,
    down_w,
    final_gain,
    score_w,
):
    token_rows = resid.shape[0]
    attn = attend_prompt(
        queries, prefix_pool, page_table[0], prompt_len[0], tail_pool, tail_len[0], new_kv
    )
    partial_value = jnp.dot(attn, out_w, preferred_element_type=jnp.float32)
    mixed = lax.psum(partial_value.astype(jnp.bfloat16), "blk").astype(jnp.float32)
    middle = resid.astype(jnp.float32) + mixed
    normed = (
        middle
        * lax.rsqrt(jnp.mean(middle * middle, -1, keepdims=True) + EPS)
        * mlp_gain.astype(jnp.float32)
    ).astype(jnp.bfloat16)
    feat_width = gate_w.shape[0]
    units = gate_w.shape[1]
    block_index = lax.axis_index("blk")
    home_index = lax.axis_index("dp")
    feat_slice = lax.dynamic_slice_in_dim(normed, block_index * feat_width, feat_width, 1)
    middle_slice = lax.dynamic_slice_in_dim(middle, block_index * feat_width, feat_width, 1)
    piece = lax.all_gather(feat_slice, "dp", axis=0, tiled=True)
    partial_units = jnp.concatenate(
        [
            jnp.dot(piece, gate_w, preferred_element_type=jnp.float32),
            jnp.dot(piece, up_w, preferred_element_type=jnp.float32),
        ],
        axis=1,
    )
    summed = lax.psum(partial_units.astype(jnp.bfloat16), "blk").astype(jnp.float32)
    hidden = (jax.nn.silu(summed[:, :units]) * summed[:, units:]).astype(jnp.bfloat16)
    source = (migration[:, None] * NEW + jnp.arange(NEW, dtype=jnp.int32)[None, :]).reshape(-1)
    term = jnp.dot(jnp.take(hidden, source, axis=0), down_w, preferred_element_type=jnp.float32)
    local_rows = source - home_index * token_rows
    own_rows = (local_rows >= 0) & (local_rows < token_rows)
    carried = jnp.take(middle_slice, jnp.clip(local_rows, 0, token_rows - 1), axis=0)
    moved = lax.psum_scatter(
        term + jnp.where(own_rows[:, None], carried, 0.0), "dp", scatter_dimension=0, tiled=True
    )
    weighted = final_gain.astype(jnp.float32) * score_w.astype(jnp.float32)
    squares, terms = lax.psum((jnp.sum(moved * moved, -1), jnp.sum(moved * weighted, -1)), "blk")
    score = terms * lax.rsqrt(squares / D + EPS)
    return (moved.astype(jnp.bfloat16), score)


def solution(mesh):
    return jax.shard_map(
        shards,
        mesh=mesh,
        in_specs=(
            P("dp", None),
            P("dp", "blk", None),
            P("dp", None, "blk", None),
            P("dp", None, None, "blk", None),
            P("dp", None),
            P("dp"),
            P("dp", None, None, "blk", None),
            P("dp", None),
            P(),
            P("blk", None),
            P(),
            P("blk", "dp"),
            P("blk", "dp"),
            P("dp", "blk"),
            P("blk"),
            P("blk"),
        ),
        out_specs=(P("dp", "blk"), P("dp")),
        check_vma=False,
    )
```

profile of v0, /device:TPU:8, one launch (start us, length us, event | category | flops | bytes accessed | tf_op | source)
XLA Modules:
  0.0 631.7 jit_solution(11279439814743314583)
XLA Ops:
  7.2 0.8 fusion.25
  8.0 0.7 compare_and_fusion.3
  9.4 6.2 gather_fusion
  15.5 3.6 copy.69
  19.3 2.3 fusion.31
  21.6 0.5 fusion.33
  22.2 0.4 fusion.22
  22.7 2.0 broadcast_select_fusion
  24.7 1.3 copy-done.2
  26.0 0.6 fusion.32
  27.2 0.4 copy-done.4
  27.9 1.6 fusion.11
  29.8 2.0 fusion.6
  31.9 0.9 convolution_convert_fusion.2
  32.9 0.8 dynamic-slice
  33.6 102.1 %all-reduce.4.cloned.1.call-done = bf16[32,2048]{1,0:T(8,128)(2,1)} async-done(((bf16[32,2048]{1,0:T(8,128)(2,1)}), bf16[32,2048]{1,0:T(8,128)(2,1)}) %all-reduce.4.cloned.1.call-update) | async-done | bytes 131088 | tf_op jit(solution)/shard_map/psum | solution.py:96
  135.7 1.1 convert_add_fusion
  136.8 0.7 multiply_convert_fusion
  138.4 119.5 %all-gather.2.cloned.1.call-done = bf16[2048,256]{1,0:T(8,128)(2,1)} async-done(((bf16[32,256]{1,0:T(8,128)(2,1)}), bf16[2048,256]{1,0:T(8,128)(2,1)}) %all-gather.2.cloned.1.call-update) | async-done | bytes 1048592 | tf_op jit(solution)/shard_map/all_gather | solution.py:109
  257.9 1.7 convolution_convert_fusion
  259.6 1.7 convolution_convert_fusion.1
  261.3 0.9 pad_maximum_fusion
  262.4 8.6 %gather_fusion.2 = f32[2048,256]{1,0:T(8,128)} fusion(f32[32,256]{1,0:T(8,128)S(1)} %get-tuple-element.7, s32[2048]{0:T(1024)S(1)} %broadcast_clamp_fusion), kind=kCustom, calls=%fused_computation.2 | custom fusion | bytes 4202496 | tf_op jit(solution)/shard_map/jit(_take)/gather | solution.py:123
  270.9 89.1 %all-reduce.6.cloned.1.call-done = bf16[2048,192]{0,1:T(8,128)(2,1)} async-done(((bf16[2048,192]{0,1:T(8,128)(2,1)}), bf16[2048,192]{0,1:T(8,128)(2,1)}) %all-reduce.6.cloned.1.call-update) | async-done | bytes 786448 | tf_op jit(solution)/shard_map/psum | solution.py:117
  360.0 1.3 convert_element_type.59
  361.9 6.2 gather_fusion.1
  368.1 4.9 convolution_add_fusion
  372.9 0.6 copy-done.12
  373.6 226.0 %reduce-scatter.2.cloned.1.call-done = f32[32,256]{1,0:T(8,128)} async-done(((f32[2048,256]{1,0:T(8,128)}), f32[32,256]{1,0:T(8,128)}) %reduce-scatter.2.cloned.1.call-update) | async-done | bytes 32784 | tf_op jit(solution)/shard_map/reduce_scatter | solution.py:124
  599.6 1.5 multiply_reduce_fusion.1
  601.1 23.5 %all-reduce = (f32[32]{0:T(128)S(1)}, f32[32]{0:T(128)S(1)}) all-reduce(f32[32]{0:T(128)S(1)} %get-tuple-element.3, f32[32]{0:T(128)S(1)} %get-tuple-element.2), channel_id=1, replica_groups=mesh['dp'=64,'blk'=8] {'blk'}, use_global_device_ids=true, to_apply=%region_11.12 | all-reduce | flops 64 | bytes 512 | tf_op jit(solution)/shard_map/psum | solution.py:128
  624.6 0.5 rsqrt_multiply_fusion
  (66 shorter events, 3.2 us)
Async XLA Ops:
  7.2 2.2 copy-start
  7.2 128.6 %all-reduce.4.cloned.1.call-start = ((), (), s32[]{:S(2)}) async-start(), calls=%async_computation.1 | async-start | bytes 262144 | tf_op jit(solution)/shard_map/psum | solution.py:96
  15.5 3.7 copy-start.11
  15.5 3.7 copy-start.1
  19.3 2.3 copy-start.14
  19.3 2.9 copy-start.9
  24.7 1.4 copy-start.2
  26.6 1.0 copy-start.4
  27.9 3.9 copy-start.3
  29.8 105.9 %copy-start.5 = (bf16[32,2048]{1,0:T(8,128)(2,1)S(1)}, bf16[32,2048]{1,0:T(8,128)(2,1)}, u32[]{:S(2)}) copy-start(bf16[32,2048]{1,0:T(8,128)(2,1)} %param.16) | copy-start | bytes 393220
  29.8 107.7 %copy-start.10 = (s32[1024]{0:T(1024)S(1)}, s32[1024]{0:T(1024)}, u32[]{:S(2)}) copy-start(s32[1024]{0:T(1024)} %param.24) | copy-start | bytes 12292
  31.8 226.1 %copy-start.7 = (bf16[256,96]{0,1:T(8,128)(2,1)S(1)}, bf16[256,96]{0,1:T(8,128)(2,1)}, u32[]{:S(2)}) copy-start(bf16[256,96]{0,1:T(8,128)(2,1)} %param.28) | copy-start | bytes 147460
  32.8 226.8 %copy-start.8 = (bf16[256,96]{0,1:T(8,128)(2,1)S(1)}, bf16[256,96]{0,1:T(8,128)(2,1)}, u32[]{:S(2)}) copy-start(bf16[256,96]{0,1:T(8,128)(2,1)} %param.27) | copy-start | bytes 147460
  32.8 225.1 %all-gather.2.cloned.1.call-start = ((), (), s32[]{:S(2)}) async-start(), calls=%async_computation.2 | async-start | bytes 1064960 | tf_op jit(solution)/shard_map/all_gather | solution.py:109
  137.5 222.5 %all-reduce.6.cloned.1.call-start = ((), (), s32[]{:S(2)}) async-start(), calls=%async_computation.3 | async-start | bytes 1572864 | tf_op jit(solution)/shard_map/psum | solution.py:117
  262.2 337.3 %reduce-scatter.2.cloned.1.call-start = ((), (), s32[]{:S(2)}) async-start(), calls=%async_computation.4 | async-start | bytes 2129920 | tf_op jit(solution)/shard_map/reduce_scatter | solution.py:124
  361.8 6.2 copy-start.6
  372.9 0.7 copy-start.12
  372.9 0.7 copy-start.13
Sparse Core Ops, SparseCore 0:
  32.9 102.7 all-reduce.3
  138.7 119.1 all-gather.1
  262.4 97.6 all-reduce.5
  373.1 226.4 reduce-scatter.1
where the time goes:
time: 632 us
  waiting for transfers between devices  537 us (85%)
  local copies, waits for them, and re-layouts  31.4 us (5%)
  blocking collectives  23.5 us (4%)
  between operations  14.7 us (2%)
  matrix products  14.3 us (2%)
  other arithmetic  10.8 us (2%)
    reduce_scatter x1, waiting for transfers between devices, shards(): lax.psum_scatter(term + jnp.where(own_rows[:, None], carried, 0.0), 'dp',...  226 us
    all_gather x1, waiting for transfers between devices, shards(): piece = lax.all_gather(feat_slice, 'dp', axis=0, tiled=True)  120 us
    psum x1, waiting for transfers between devices, shards(): lax.psum(partial_value.astype(jnp.bfloat16), 'blk').astype(jnp.float32)  102 us
    psum x1, waiting for transfers between devices, shards(): lax.psum(partial_units.astype(jnp.bfloat16), 'blk').astype(jnp.float32)  89.1 us
    psum x1, blocking collectives, shards(): lax.psum((jnp.sum(moved * moved, -1), jnp.sum(moved * weighted, -1)), 'blk')  23.5 us
  transfers between devices with their start and end apart: 4, of which 4 were waited for; matrix products, arithmetic and copies ran while one was open for 2% of the time, Pallas kernels for 0%

commit v1 on v0

--- a/solution.py
+++ b/solution.py
@@ -114,7 +114,9 @@
         ],
         axis=1,
     )
-    summed = lax.psum(partial_units.astype(jnp.bfloat16), "blk").astype(jnp.float32)
+    summed = jnp.sum(lax.all_gather(partial_units.astype(jnp.bfloat16), "blk"), axis=0).astype(
+        jnp.float32
+    )
     hidden = (jax.nn.silu(summed[:, :units]) * summed[:, units:]).astype(jnp.bfloat16)
     source = (migration[:, None] * NEW + jnp.arange(NEW, dtype=jnp.int32)[None, :]).reshape(-1)
     term = jnp.dot(jnp.take(hidden, source, axis=0), down_w, preferred_element_type=jnp.float32)

time: 632 us -> 641 us (1.014)
    all_gather x0 -> x1, waiting for transfers between devices: none -> 91.5 us  [shards(): lax.all_gather(partial_units.astype(jnp.bfloat16), 'blk')]
    psum x1 -> x0, waiting for transfers between devices: 89.1 us -> none  [shards(): lax.psum(partial_units.astype(jnp.bfloat16), 'blk').astype(jnp.float32)]
where the time goes in v1:
time: 641 us; the launch traced here: 640 us
  waiting for transfers between devices  540 us (84%)
  local copies, waits for them, and re-layouts  32.6 us (5%)
  blocking collectives  23.5 us (4%)
  other arithmetic  15 us (2%)
  between operations  14.7 us (2%)
  matrix products  14.3 us (2%)
    reduce_scatter x1, waiting for transfers between devices, shards(): lax.psum_scatter(term + jnp.where(own_rows[:, None], carried, 0.0), 'dp',...  226 us
    all_gather x1, waiting for transfers between devices, shards(): piece = lax.all_gather(feat_slice, 'dp', axis=0, tiled=True)  120 us
    psum x1, waiting for transfers between devices, shards(): lax.psum(partial_value.astype(jnp.bfloat16), 'blk').astype(jnp.float32)  102 us
    all_gather x1, waiting for transfers between devices, shards(): lax.all_gather(partial_units.astype(jnp.bfloat16), 'blk')  91.5 us
    psum x1, blocking collectives, shards(): lax.psum((jnp.sum(moved * moved, -1), jnp.sum(moved * weighted, -1)), 'blk')  23.5 us
  transfers between devices with their start and end apart: 4, of which 4 were waited for; matrix products, arithmetic and copies ran while one was open for 2% of the time, Pallas kernels for 0%

profile of v1, /device:TPU:8, one launch (start us, length us, event | category | flops | bytes accessed | tf_op | source)
XLA Modules:
  0.0 640.1 jit_solution(4874431722663508482)
XLA Ops:
  7.2 0.8 fusion.27
  8.0 0.7 compare_and_fusion.3
  9.4 6.2 gather_fusion
  15.5 3.6 copy.67
  19.3 2.3 fusion.33
  21.6 0.5 fusion.35
  22.2 0.4 fusion.24
  22.7 2.0 broadcast_select_fusion
  24.7 1.3 copy-done.2
  26.0 0.6 fusion.34
  27.9 1.6 fusion.13
  29.8 2.0 fusion.8
  31.9 0.9 convolution_convert_fusion.2
  32.9 0.8 dynamic-slice
  33.6 102.1 %all-reduce.3.cloned.1.call-done = bf16[32,2048]{1,0:T(8,128)(2,1)} async-done(((bf16[32,2048]{1,0:T(8,128)(2,1)}), bf16[32,2048]{1,0:T(8,128)(2,1)}) %all-reduce.3.cloned.1.call-update) | async-done | bytes 131088 | tf_op jit(solution)/shard_map/psum | solution.py:96
  135.7 1.1 convert_add_fusion
  136.8 0.7 multiply_convert_fusion
  137.6 120.4 %all-gather.3.cloned.1.call-done = bf16[2048,256]{1,0:T(8,128)(2,1)} async-done(((bf16[32,256]{1,0:T(8,128)(2,1)}), bf16[2048,256]{1,0:T(8,128)(2,1)}) %all-gather.3.cloned.1.call-update) | async-done | bytes 1048592 | tf_op jit(solution)/shard_map/all_gather | solution.py:109
  257.9 1.7 fusion.2
  259.6 1.7 fusion.3
  261.3 1.0 pad_maximum_fusion
  263.3 8.6 %gather_fusion.2 = f32[2048,256]{1,0:T(8,128)} fusion(f32[32,256]{1,0:T(8,128)S(1)} %get-tuple-element.7, s32[2048]{0:T(1024)S(1)} %broadcast_clamp_fusion), kind=kCustom, calls=%fused_computation.2 | custom fusion | bytes 4202496 | tf_op jit(solution)/shard_map/jit(_take)/gather | solution.py:125
  271.8 91.5 %all-gather.5.cloned.1.call-done = bf16[8,2048,192]{1,2,0:T(8,128)(2,1)} async-done(((bf16[1,2048,192]{1,2,0:T(8,128)(2,1)}), bf16[8,2048,192]{1,2,0:T(8,128)(2,1)}) %all-gather.5.cloned.1.call-update) | async-done | bytes 6291472 | tf_op jit(solution)/shard_map/all_gather | solution.py:117
  363.4 5.1 reduce_sum.70
  368.5 1.4 copy.84
  370.5 6.2 gather_fusion.1
  376.7 4.9 convolution_add_fusion
  381.6 0.6 copy-done.12
  382.2 225.8 %reduce-scatter.2.cloned.1.call-done = f32[32,256]{1,0:T(8,128)} async-done(((f32[2048,256]{1,0:T(8,128)}), f32[32,256]{1,0:T(8,128)}) %reduce-scatter.2.cloned.1.call-update) | async-done | bytes 32784 | tf_op jit(solution)/shard_map/reduce_scatter | solution.py:126
  608.0 1.5 multiply_reduce_fusion.1
  609.6 23.5 %all-reduce = (f32[32]{0:T(128)S(1)}, f32[32]{0:T(128)S(1)}) all-reduce(f32[32]{0:T(128)S(1)} %get-tuple-element.3, f32[32]{0:T(128)S(1)} %get-tuple-element.2), channel_id=1, replica_groups=mesh['dp'=64,'blk'=8] {'blk'}, use_global_device_ids=true, to_apply=%region_11.12 | all-reduce | flops 64 | bytes 512 | tf_op jit(solution)/shard_map/psum | solution.py:130
  633.1 0.5 rsqrt_multiply_fusion
  (67 shorter events, 3.6 us)
Async XLA Ops:
  7.2 2.2 copy-start
  7.2 128.5 %all-reduce.3.cloned.1.call-start = ((), (), s32[]{:S(2)}) async-start(), calls=%async_computation.1 | async-start | bytes 262144 | tf_op jit(solution)/shard_map/psum | solution.py:96
  15.5 3.7 copy-start.11
  15.5 3.7 copy-start.1
  19.3 2.3 copy-start.14
  19.3 2.9 copy-start.9
  24.7 1.4 copy-start.2
  26.6 1.0 copy-start.4
  27.9 3.9 copy-start.3
  29.8 105.9 %copy-start.5 = (bf16[32,2048]{1,0:T(8,128)(2,1)S(1)}, bf16[32,2048]{1,0:T(8,128)(2,1)}, u32[]{:S(2)}) copy-start(bf16[32,2048]{1,0:T(8,128)(2,1)} %param.16) | copy-start | bytes 393220
  29.8 228.1 %copy-start.7 = (bf16[256,96]{0,1:T(8,128)(2,1)S(1)}, bf16[256,96]{0,1:T(8,128)(2,1)}, u32[]{:S(2)}) copy-start(bf16[256,96]{0,1:T(8,128)(2,1)} %param.27) | copy-start | bytes 147460
  31.8 227.8 %copy-start.8 = (bf16[256,96]{0,1:T(8,128)(2,1)S(1)}, bf16[256,96]{0,1:T(8,128)(2,1)}, u32[]{:S(2)}) copy-start(bf16[256,96]{0,1:T(8,128)(2,1)} %param.28) | copy-start | bytes 147460
  32.8 225.1 %all-gather.3.cloned.1.call-start = ((), (), s32[]{:S(2)}) async-start(), calls=%async_computation.2 | async-start | bytes 1064960 | tf_op jit(solution)/shard_map/all_gather | solution.py:109
  137.5 225.9 %all-gather.5.cloned.1.call-start = ((), (), s32[]{:S(2)}) async-start(), calls=%async_computation.3 | async-start | bytes 7077888 | tf_op jit(solution)/shard_map/all_gather | solution.py:117
  259.6 2.8 copy-start.10
  262.3 345.7 %reduce-scatter.2.cloned.1.call-start = ((), (), s32[]{:S(2)}) async-start(), calls=%async_computation.4 | async-start | bytes 2129920 | tf_op jit(solution)/shard_map/reduce_scatter | solution.py:126
  370.4 6.2 copy-start.6
  381.5 0.7 copy-start.12
  381.5 0.7 copy-start.13
Sparse Core Ops, SparseCore 0:
  32.9 102.7 all-reduce.2
  138.7 119.1 all-gather.2
  262.4 100.8 all-gather.4
  381.7 226.3 reduce-scatter.1
